TPU v7x, 32 devices: a whole 2x2x4 slice. The times are simulated.
32 devices in a mesh: replica: 8 (over y, x, core), group: 4 (over z).
Axes of the slice: x: 2, y: 2, z: 4, core: 2. Of those that a mesh axis runs over, the one named last changes fastest.
Arguments:
- inputs: bfloat16 [8, 512, 2048], P('replica', 'group'), may hold values from -6 to 6
- seq_lengths: int32 [8], P('replica'), may hold values from 128 to 512, as said below
- bucket_ids: int32 [1023], replicated, may hold values from 0 to 31, as said below
- norm1_gain: bfloat16 [2048], P('group'), may hold values from 0.25 to 1.75
- w_query: bfloat16 [2048, 2048], P(None, 'group'), may hold values from -0.0625 to 0.0625
- w_key: bfloat16 [2048, 2048], P(None, 'group'), may hold values from -0.0625 to 0.0625
- w_value: bfloat16 [2048, 2048], P(None, 'group'), may hold values from -0.125 to 0.125
- w_attn_out: bfloat16 [2048, 2048], P('group'), may hold values from -0.5 to 0.5
- bias_table: bfloat16 [32, 32], P(None, 'group'), may hold values from -4 to 4
- norm2_gain: bfloat16 [2048], P('group'), may hold values from 0.25 to 1.75
- w_gate: bfloat16 [2048, 5120], P(None, 'group'), may hold values from -0.125 to 0.125
- w_up: bfloat16 [2048, 5120], P(None, 'group'), may hold values from -0.125 to 0.125
- w_ffn_out: bfloat16 [5120, 2048], P('group'), may hold values from -0.078125 to 0.078125
- cotangent: bfloat16 [8, 512, 2048], P('replica', 'group'), may hold values from -6 to 6
Outputs:
- result: bfloat16 [8, 512, 2048], P('replica', 'group')
- input_grad: bfloat16 [8, 512, 2048], P('replica', 'group')
- norm1_gain_grad: float32 [2048], P('group')
- query_grad: float32 [2048, 2048], P(None, 'group')
- key_grad: float32 [2048, 2048], P(None, 'group')
- value_grad: float32 [2048, 2048], P(None, 'group')
- attn_out_grad: float32 [2048, 2048], P('group')
- bias_table_grad: float32 [32, 32], P(None, 'group')
- norm2_gain_grad: float32 [2048], P('group')
- gate_grad: float32 [2048, 5120], P(None, 'group')
- up_grad: float32 [2048, 5120], P(None, 'group')
- ffn_out_grad: float32 [5120, 2048], P('group')
Inputs may be any that keep to these rules, and one draw needn't show every extreme that they name: `seq_lengths`: one sequence has exactly 512 valid positions and another exactly 128. `bucket_ids`: entry 511 + o is the bucket of the offset o = key position - query position; every bucket occurs.
All inputs are finite; a program needn't handle non-finite values.
Results may differ from a plain program's by a relative error of at most 0.02.
Values may be sent and summed in bfloat16 or wider, within the bound.
A program may use at most 448 MiB of HBM per device.

v0:
```python
import jax
import jax.numpy as jnp
from jax import lax
from jax.sharding import PartitionSpec as P

epsilon = 1e-06
negative = -1000000000.0
highest = lax.Precision.HIGHEST
head_dim = 64


def rms_scale(values, gain):
    return values * lax.rsqrt(jnp.mean(values * values, axis=-1, keepdims=True) + epsilon) * gain


def gated_gelu(gate_pre, up_pre):
    return jax.nn.gelu(gate_pre, approximate=True) * up_pre


def rows_dot(left, right):
    return lax.dot_general(
        left, right, (((0,), (0,)), ((), ())), preferred_element_type=jnp.float32
    )


def cols_dot(left, right):
    return lax.dot_general(
        left, right, (((1,), (1,)), ((), ())), preferred_element_type=jnp.float32
    )


def plain_dot(left, right):
    return jnp.dot(left, right, preferred_element_type=jnp.float32)


def spread_offsets(vector, row_count, col_count):
    span_width = row_count + col_count + 1
    block_heads = vector.shape[0]
    tiled_rows = jnp.broadcast_to(vector[:, None, :], (block_heads, row_count, span_width))
    flattened = tiled_rows.reshape(block_heads, row_count * span_width)[
        :, : row_count * (span_width - 1)
    ]
    return flattened.reshape(block_heads, row_count, span_width - 1)[:, :, row_count:]


def fold_offsets(matrix):
    block_heads, row_count, col_count = matrix.shape
    padded = jnp.pad(matrix, ((0, 0), (0, 0), (row_count, 0)))
    flattened = jnp.pad(
        padded.reshape(block_heads, row_count * (row_count + col_count)), ((0, 0), (0, row_count))
    )
    sums_all = flattened.reshape(block_heads, row_count, row_count + col_count + 1).sum(axis=1)
    return sums_all[:, 1 : row_count + col_count]


def heads(matrix):
    return matrix.reshape(matrix.shape[0], -1, head_dim)


def local(
    inputs,
    seq_lengths,
    bucket_ids,
    norm1_gain,
    w_query,
    w_key,
    w_value,
    w_attn_out,
    bias_table,
    norm2_gain,
    w_gate,
    w_up,
    w_ffn_out,
    cotangent,
):
    group = lax.axis_index("group")
    rows = inputs.shape[1]
    length = seq_lengths[0]
    total = rows * lax.axis_size("group")
    start = group * rows
    valid = jnp.arange(total) < length

    def gather(values):
        return lax.all_gather(values, "group", axis=0, tiled=True)

    def scatter(values):
        return lax.psum_scatter(
            values.astype(jnp.bfloat16), "group", scatter_dimension=0, tiled=True
        ).astype(jnp.float32)

    x_all_low = gather(inputs[0])
    g_all = jnp.where(valid[:, None], gather(cotangent[0]), jnp.bfloat16(0))
    gains = lax.all_gather(jnp.stack([norm1_gain, norm2_gain]), "group", axis=1, tiled=True)
    gains = gains.astype(jnp.float32)
    gain_first, gain_second = (gains[0], gains[1])
    x_local = inputs[0].astype(jnp.float32)
    normed_one = rms_scale(x_all_low.astype(jnp.float32), gain_first).astype(jnp.bfloat16)
    query = plain_dot(normed_one, w_query).astype(jnp.bfloat16)
    key = plain_dot(normed_one, w_key).astype(jnp.bfloat16)
    value = plain_dot(normed_one, w_value).astype(jnp.bfloat16)
    buckets = bias_table.shape[0]
    one_hot = (bucket_ids[:, None] == jnp.arange(buckets)[None, :]).astype(jnp.float32)
    per_offset = jnp.dot(one_hot, bias_table.astype(jnp.float32), precision=highest)
    bias = spread_offsets(jnp.pad(per_offset.T, ((0, 0), (1, 1))), total, total)
    scores = jnp.einsum(
        "qhd,khd->hqk", heads(query), heads(key), preferred_element_type=jnp.float32
    )
    scores = jnp.where(valid[None, None, :], scores + bias, negative)
    probs = jax.nn.softmax(scores, axis=-1)
    probs_low = probs.astype(jnp.bfloat16)
    attended = jnp.einsum(
        "hqk,khd->qhd", probs_low, heads(value), preferred_element_type=jnp.float32
    )
    attended = attended.reshape(total, -1).astype(jnp.bfloat16)
    middle = x_local + scatter(plain_dot(attended, w_attn_out))
    normed_two = gather(rms_scale(middle, gain_second).astype(jnp.bfloat16))
    gate_pre = plain_dot(normed_two, w_gate)
    up_pre = plain_dot(normed_two, w_up)
    hidden_low = gated_gelu(gate_pre, up_pre).astype(jnp.bfloat16)
    grad_hidden = cols_dot(g_all, w_ffn_out)
    _, pull_gelu = jax.vjp(gated_gelu, gate_pre, up_pre)
    grad_gate, grad_up = pull_gelu(grad_hidden)
    grad_gate = grad_gate.astype(jnp.bfloat16)
    grad_up = grad_up.astype(jnp.bfloat16)
    grad_normed_two = scatter(cols_dot(grad_gate, w_gate) + cols_dot(grad_up, w_up))
    ffn_out_grad = rows_dot(hidden_low, g_all)
    gate_grad = rows_dot(normed_two, grad_gate)
    up_grad = rows_dot(normed_two, grad_up)

    def total_sum(values):
        return lax.psum(values.astype(jnp.bfloat16), "replica").astype(jnp.float32)

    ffn_out_grad, gate_grad, up_grad = (
        total_sum(ffn_out_grad),
        total_sum(gate_grad),
        total_sum(up_grad),
    )
    result = (middle + scatter(plain_dot(hidden_low, w_ffn_out))).astype(jnp.bfloat16)
    row_valid = start + jnp.arange(rows) < length
    g_local = jnp.where(row_valid[:, None], cotangent[0], jnp.bfloat16(0)).astype(jnp.float32)
    _, pull_two = jax.vjp(rms_scale, middle, gain_second)
    grad_mid_norm, gain_two_grad = pull_two(grad_normed_two)
    grad_middle = g_local + grad_mid_norm
    grad_branch = gather(grad_middle.astype(jnp.bfloat16))
    attn_out_grad = rows_dot(attended, grad_branch)
    grad_attended = cols_dot(grad_branch, w_attn_out).astype(jnp.bfloat16)
    grad_probs = jnp.einsum(
        "qhd,khd->hqk", heads(grad_attended), heads(value), preferred_element_type=jnp.float32
    )
    inner_sum = jnp.sum(probs * grad_probs, axis=-1, keepdims=True)
    grad_scores = (probs * (grad_probs - inner_sum)).astype(jnp.bfloat16)

    def merge(values):
        return values.reshape(total, -1).astype(jnp.bfloat16)

    grad_query = merge(
        jnp.einsum("hqk,khd->qhd", grad_scores, heads(key), preferred_element_type=jnp.float32)
    )
    grad_key = merge(
        jnp.einsum("hqk,qhd->khd", grad_scores, heads(query), preferred_element_type=jnp.float32)
    )
    grad_value = merge(
        jnp.einsum(
            "hqk,qhd->khd", probs_low, heads(grad_attended), preferred_element_type=jnp.float32
        )
    )
    offset_sums = fold_offsets(grad_scores.astype(jnp.float32))
    table_grad = jnp.dot(offset_sums, one_hot, precision=highest).T
    query_grad = rows_dot(normed_one, grad_query)
    key_grad = rows_dot(normed_one, grad_key)
    value_grad = rows_dot(normed_one, grad_value)
    grad_normed_one = scatter(
        cols_dot(grad_query, w_query) + cols_dot(grad_key, w_key) + cols_dot(grad_value, w_value)
    )
    query_grad, key_grad, value_grad, attn_out_grad = (
        total_sum(query_grad),
        total_sum(key_grad),
        total_sum(value_grad),
        total_sum(attn_out_grad),
    )
    table_grad = lax.psum(table_grad, "replica")
    _, pull_one = jax.vjp(rms_scale, x_local, gain_first)
    grad_in_norm, gain_one_grad = pull_one(grad_normed_one)
    input_grad = (grad_middle + grad_in_norm).astype(jnp.bfloat16)
    gain_sums = lax.psum(jnp.stack([gain_one_grad, gain_two_grad]), ("replica", "group"))
    width = norm1_gain.shape[0]
    gain_sums = lax.dynamic_slice_in_dim(gain_sums, group * width, width, axis=1)
    return (
        result[None],
        input_grad[None],
        gain_sums[0],
        query_grad,
        key_grad,
        value_grad,
        attn_out_grad,
        table_grad,
        gain_sums[1],
        gate_grad,
        up_grad,
        ffn_out_grad,
    )


def solution(mesh):
    placed = (
        P("replica", "group", None),
        P("replica"),
        P(),
        P("group"),
        P(None, "group"),
        P(None, "group"),
        P(None, "group"),
        P("group", None),
        P(None, "group"),
        P("group"),
        P(None, "group"),
        P(None, "group"),
        P("group", None),
        P("replica", "group", None),
    )
    return jax.shard_map(
        local,
        mesh=mesh,
        in_specs=placed,
        out_specs=(
            P("replica", "group", None),
            P("replica", "group", None),
            P("group"),
            P(None, "group"),
            P(None, "group"),
            P(None, "group"),
            P("group", None),
            P(None, "group"),
            P("group"),
            P(None, "group"),
            P(None, "group"),
            P("group", None),
        ),
        check_vma=False,
    )
```

profile of v0, /device:TPU:0, one launch (start us, length us, event | category | flops | bytes accessed | tf_op | source)
XLA Modules:
  0.0 854.6 jit_solution(4421860915725678596)
XLA Ops:
  11.1 7.7 broadcast_in_dim.67
  18.7 25.5 %reshape.150 = f32[4198400]{0:T(1024)} reshape(f32[8,512,1025]{2,1,0:T(8,128)} %broadcast_in_dim.67) | data formatting | bytes 33587200
  44.2 16.5 %reshape.135 = f32[8,524800]{1,0:T(8,128)} reshape(f32[4198400]{0:T(1024)} %reshape.150) | data formatting | bytes 33587200 | tf_op jit(solution)/shard_map/reshape | solution.py:40
  60.7 5.8 slice-done
  66.5 16.0 %copy.45 = f32[1,8,512,1024]{3,2,1,0:T(8,128)S(1)} copy(f32[1,8,512,1024]{3,1,2,0:T(8,128)S(1)} %bitcast.126) | data formatting | bytes 33554432
  82.5 4.4 slice.30
  86.9 9.1 %copy.40 = f32[8,512,512]{1,2,0:T(8,128)} copy(f32[8,512,512]{2,1,0:T(8,128)} %slice.30) | data formatting | bytes 16777216
  96.0 14.0 %all_gather.16 = bf16[2,2048]{1,0:T(2,128)(2,1)S(1)} all-gather(bf16[2,512]{1,0:T(2,128)(2,1)S(1)} %pad_maximum_fusion.1), channel_id=1, replica_groups=mesh['replica'=8,'group'=4] {'group'}, dimensions={1}, use_global_device_ids=true | all-gather | bytes 10240 | tf_op jit(solution)/shard_map/all_gather | solution.py:93
  110.1 2.2 fusion.1
  112.4 3.8 convolution_convert_fusion.13
  116.2 1.4 convolution_convert_fusion.12
  118.6 1.9 add_select_fusion
  120.6 5.0 fusion.52
  126.7 1.4 convolution_convert_fusion.14
  128.1 8.1 fusion.15
  136.3 2.6 convolution_convert_fusion.8
  138.9 43.8 %reduce-scatter.5.cloned.1.call-done = bf16[128,2048]{1,0:T(8,128)(2,1)} async-done(((bf16[512,2048]{1,0:T(8,128)(2,1)}), bf16[128,2048]{1,0:T(8,128)(2,1)}) %reduce-scatter.5.cloned.1.call-update) | async-done | bytes 524304 | tf_op jit(solution)/shard_map/reduce_scatter | solution.py:87
  184.0 2.0 multiply_convert_fusion.3
  186.9 44.6 %all-gather.7.cloned.1.call-done = bf16[512,2048]{1,0:T(8,128)(2,1)} async-done(((bf16[128,2048]{1,0:T(8,128)(2,1)}), bf16[512,2048]{1,0:T(8,128)(2,1)}) %all-gather.7.cloned.1.call-update) | async-done | bytes 2097168 | tf_op jit(solution)/shard_map/all_gather | solution.py:84
  231.5 7.6 fusion.53
  239.1 7.1 fusion.54
  246.2 31.5 %all-gather.13.cloned.1.call-done = bf16[1,512,2048]{2,1,0:T(8,128)(2,1)} async-done(((bf16[1,128,2048]{2,1,0:T(8,128)(2,1)}), bf16[1,512,2048]{2,1,0:T(8,128)(2,1)}) %all-gather.13.cloned.1.call-update) | async-done | bytes 2097168 | tf_op jit(solution)/shard_map/all_gather | solution.py:84
  277.7 10.4 %multiply_convert_fusion.1 = (bf16[512,1280]{1,0:T(8,128)(2,1)S(1)}, bf16[512,1280]{1,0:T(8,128)(2,1)S(1)}, bf16[512,1280]{1,0:T(8,128)(2,1)}) fusion(f32[512,1280]{1,0:T(8,128)} %fusion.53, f32[512,1280]{1,0:T(8,128)} %fusion.54, bf16[1280,2048]{1,0:T(8,128)(2,1)} %param.26, bf16[1,512,2048]{2,1,0:T(8,128)(2,1)} %all-gather.13.cloned.1.call-done, ...), kind=kOutput, calls=%fused_computation.34 | convolution fusion | flops 2702442496 | bytes 16515584 | tf_op jit(solution)/shard_map/dot_general | solution.py:27
  288.1 5.8 fusion.55
  293.9 6.7 add_convert_fusion.1
  300.7 42.6 %reduce-scatter.9.cloned.1.call-done = bf16[128,2048]{1,0:T(8,128)(2,1)} async-done(((bf16[512,2048]{1,0:T(8,128)(2,1)}), bf16[128,2048]{1,0:T(8,128)(2,1)}) %reduce-scatter.9.cloned.1.call-update) | async-done | bytes 524304 | tf_op jit(solution)/shard_map/reduce_scatter | solution.py:87
  343.3 1.7 fusion.25
  345.0 2.4 fusion.43
  347.7 45.2 %all-gather.9.cloned.1.call-done = bf16[512,2048]{1,0:T(8,128)(2,1)} async-done(((bf16[128,2048]{1,0:T(8,128)(2,1)}), bf16[512,2048]{1,0:T(8,128)(2,1)}) %all-gather.9.cloned.1.call-update) | async-done | bytes 2097168 | tf_op jit(solution)/shard_map/all_gather | solution.py:84
  392.9 3.7 convolution_convert_fusion.11
  396.5 8.2 fusion.18
  404.8 4.8 multiply_reduce_fusion
  410.6 2.5 multiply_convert_fusion
  413.2 1.4 convolution_convert_fusion.9
  416.8 1.3 fusion.57
  418.4 1.3 fusion.56
  419.9 2.7 add_convert_fusion
  423.1 7.1 convolution_convert_fusion.7
  430.3 7.3 convolution_convert_fusion.1
  437.7 4.7 convolution_convert_fusion.2
  442.4 4.8 convolution_convert_fusion
  447.1 6.6 copy.41
  453.7 6.7 pad_bitcast_fusion
  460.5 11.7 %copy.43 = bf16[1,8,512,1024]{3,1,2,0:T(8,128)(2,1)} copy(bf16[1,8,512,1024]{3,2,1,0:T(8,128)(2,1)} %pad_bitcast_fusion) | data formatting | bytes 16777216
  472.1 2.6 convolution_convert_fusion.3
  474.8 2.9 convolution_convert_fusion.4
  477.7 2.9 convolution_convert_fusion.5
  480.5 2.9 convolution_convert_fusion.6
  483.4 10.1 %pad_convert_fusion = f32[8,524800]{1,0:T(8,128)} fusion(bf16[8,524288]{1,0:T(8,128)(2,1)} %bitcast.132), kind=kLoop, calls=%fused_computation.2 | loop fusion | flops 4198400 | bytes 25182208 | tf_op jit(solution)/shard_map/reshape | solution.py:52
  493.5 12.7 %reshape.152 = f32[4198400]{0:T(1024)} reshape(f32[8,524800]{1,0:T(8,128)} %pad_convert_fusion) | data formatting | bytes 33587200
  506.2 31.4 %reshape.144 = f32[8,512,1025]{2,1,0:T(8,128)} reshape(f32[4198400]{0:T(1024)} %reshape.152) | data formatting | bytes 33587200 | tf_op jit(solution)/shard_map/reshape | solution.py:52
  537.6 7.7 reduce_sum.104
  545.7 13.8 %psum.68 = f32[32,8]{0,1:T(8,128)} all-reduce(f32[32,8]{0,1:T(8,128)S(1)} %fusion.35), channel_id=1, replica_groups=mesh['replica'=8,'group'=4] {'replica'}, use_global_device_ids=true, to_apply=%region_20.21 | all-reduce | flops 256 | bytes 2048 | tf_op jit(solution)/shard_map/psum | solution.py:181
  559.5 1.6 fusion.26
  561.2 39.4 %psum.63 = f32[2,2048]{1,0:T(2,128)S(1)} all-reduce(f32[2,2048]{1,0:T(2,128)S(1)} %pad_maximum_fusion), channel_id=1, replica_groups=mesh['replica'=8,'group'=4] {'replica','group'}, use_global_device_ids=true, to_apply=%region_14.15 | all-reduce | flops 4096 | bytes 32768 | tf_op jit(solution)/shard_map/psum | solution.py:185
  601.3 3.3 fusion.34
  604.5 214.6 %all-reduce.6.cloned.1.call-done = (bf16[2048,512]{1,0:T(8,128)(2,1)}, bf16[2048,512]{1,0:T(8,128)(2,1)}, bf16[2048,512]{1,0:T(8,128)(2,1)}, bf16[512,2048]{1,0:...) async-done(((bf16[2048,512]{1,0:T(8,128)(2,1)}, bf16[2048,512]{1,0:T(8,128)(2,1)}, bf16[2048,512]{1,0:T(8,128)(2,1)}, ...) | async-done | bytes 24117264 | tf_op jit(solution)/shard_map/psum | solution.py:131
  819.1 7.9 convert_element_type.212
  827.0 4.9 convert_element_type.214
  831.9 5.5 convert_element_type.216
  837.4 2.6 convert_element_type.204
  840.1 2.6 convert_element_type.206
  842.7 2.6 convert_element_type.208
  845.3 2.5 convert_element_type.210
  (131 shorter events, 13.3 us)
Async XLA Ops:
  7.2 129.1 %copy-start = (bf16[512,2048]{1,0:T(8,128)(2,1)S(1)}, bf16[512,2048]{1,0:T(8,128)(2,1)}, u32[]{:S(2)}) copy-start(bf16[512,2048]{1,0:T(8,128)(2,1)} %param.21) | copy-start | bytes 6291460
  7.2 102.9 %all-gather.11.cloned.1.call-start = ((), (), s32[]{:S(2)}) async-start(), calls=%async_computation.10 | async-start | bytes 2621440 | tf_op jit(solution)/shard_map/all_gather | solution.py:84
  7.9 174.8 %reduce-scatter.5.cloned.1.call-start = ((), (), s32[]{:S(2)}) async-start(), calls=%async_computation.4 | async-start | bytes 2621440 | tf_op jit(solution)/shard_map/reduce_scatter | solution.py:87
  60.7 5.8 slice-start
  110.1 6.0 copy-start.21
  112.4 3.8 copy-start.19
  112.4 6.1 slice-start.3
  116.2 1.5 copy-start.17
  116.2 2.4 slice-start.4
  117.7 0.8 copy-start.15
  120.6 6.1 copy-start.3
  120.6 6.1 copy-start.9
  128.1 8.1 copy-start.31
  136.2 2.6 copy-start.29
  136.3 46.4 %copy-start.4 = (bf16[1,128,2048]{2,1,0:T(8,128)(2,1)S(1)}, bf16[1,128,2048]{2,1,0:T(8,128)(2,1)}, u32[]{:S(2)}) copy-start(bf16[1,128,2048]{2,1,0:T(8,128)(2,1)} %param.14) | copy-start | bytes 1572868
  138.9 92.6 %all-gather.7.cloned.1.call-start = ((), (), s32[]{:S(2)}) async-start(), calls=%async_computation.5 | async-start | bytes 2621440 | tf_op jit(solution)/shard_map/all_gather | solution.py:84
  186.1 91.6 %all-gather.13.cloned.1.call-start = ((), (), s32[]{:S(2)}) async-start(), calls=%async_computation.11 | async-start | bytes 2621440 | tf_op jit(solution)/shard_map/all_gather | solution.py:84
  186.7 156.6 %reduce-scatter.9.cloned.1.call-start = ((), (), s32[]{:S(2)}) async-start(), calls=%async_computation.7 | async-start | bytes 2621440 | tf_op jit(solution)/shard_map/reduce_scatter | solution.py:87
  231.5 7.6 copy-start.24
  288.1 5.8 copy-start.35
  288.1 5.8 copy-start.34
  293.9 49.4 %copy-start.5 = (bf16[128,2048]{1,0:T(8,128)(2,1)S(1)}, bf16[128,2048]{1,0:T(8,128)(2,1)}, u32[]{:S(2)}) copy-start(bf16[128,2048]{1,0:T(8,128)(2,1)} %reduce-scatter.5.cloned.1.call-done) | copy-start | bytes 1572868
  300.6 92.2 %all-gather.9.cloned.1.call-start = ((), (), s32[]{:S(2)}) async-start(), calls=%async_computation.8 | async-start | bytes 2621440 | tf_op jit(solution)/shard_map/all_gather | solution.py:84
  347.4 212.1 %reduce-scatter.11.cloned.1.call-start = ((), (), s32[]{:S(2)}) async-start(), calls=%async_computation.9 | async-start | bytes 2621440 | tf_op jit(solution)/shard_map/reduce_scatter | solution.py:87
  396.5 8.2 copy-start.32
  396.5 8.2 copy-start.33
  404.8 4.9 slice-start.1
  404.8 5.8 slice-start.2
  410.6 2.5 copy-start.18
  413.2 2.0 copy-start.2
  413.2 2.0 copy-start.16
  415.2 1.6 copy-start.22
  416.8 1.6 copy-start.23
  418.4 1.6 copy-start.10
  422.7 178.5 %reduce-scatter.7.cloned.1.call-start = ((), (), s32[]{:S(2)}) async-start(), calls=%async_computation.6 | async-start | bytes 2621440 | tf_op jit(solution)/shard_map/reduce_scatter | solution.py:87
  430.3 388.8 %all-reduce.6.cloned.1.call-start = ((), (), s32[]{:S(2)}) async-start(), calls=%async_computation.12 | async-start | bytes 48234496 | tf_op jit(solution)/shard_map/psum | solution.py:131
  430.3 7.3 copy-start.25
  430.3 7.3 copy-start.36
  437.7 4.7 copy-start.26
  437.7 4.7 copy-start.37
  460.5 11.7 %copy-start.27 = (bf16[512,2048]{1,0:T(8,128)(2,1)S(1)}, bf16[512,2048]{1,0:T(8,128)(2,1)}, u32[]{:S(2)}) copy-start(bf16[512,2048]{1,0:T(8,128)(2,1)} %all-gather.9.cloned.1.call-done) | copy-start | bytes 6291460
  460.5 11.7 %copy-start.30 = (bf16[8,64,512]{2,1,0:T(8,128)(2,1)S(1)}, bf16[8,64,512]{2,1,0:T(8,128)(2,1)}, u32[]{:S(2)}) copy-start(bf16[8,64,512]{2,1,0:T(8,128)(2,1)} %copy-done.29) | copy-start | bytes 1572868
  472.1 2.6 copy-start.20
  537.6 7.7 copy-start.28
  537.6 63.6 %copy-start.7 = (bf16[128,2048]{1,0:T(8,128)(2,1)S(1)}, bf16[128,2048]{1,0:T(8,128)(2,1)}, u32[]{:S(2)}) copy-start(bf16[128,2048]{1,0:T(8,128)(2,1)} %reduce-scatter.9.cloned.1.call-done) | copy-start | bytes 1572868
  537.6 63.6 %copy-start.8 = (bf16[1,128,2048]{2,1,0:T(8,128)(2,1)S(1)}, bf16[1,128,2048]{2,1,0:T(8,128)(2,1)}, u32[]{:S(2)}) copy-start(bf16[1,128,2048]{2,1,0:T(8,128)(2,1)} %param.27) | copy-start | bytes 1572868
  819.1 7.9 copy-start.6
  819.1 12.8 %slice-start.5 = ((s8[5242880]{0:T(1024)(128)(4,1)}), s8[4194304]{0:T(1024)(128)(4,1)S(1)}, s32[]{:S(2)}) async-start(s8[5242880]{0:T(1024)(128)(4,1)} %bitcast.133), calls=%async_computation.18 | async-start | bytes 8388608
  827.0 4.9 slice-start.6
  831.9 5.5 copy-start.14
  837.4 2.6 copy-start.13
  840.0 2.6 copy-start.12
  842.7 2.6 copy-start.11
  845.3 2.5 copy-start.1
Sparse Core Ops, SparseCore 0:
  9.6 48.6 all-gather.10
  139.0 43.6 reduce-scatter.4
  186.2 45.2 all-gather.6
  233.0 44.6 all-gather.12
  300.8 42.4 reduce-scatter.8
  347.6 45.2 all-gather.8
  422.8 42.5 reduce-scatter.10
  468.4 43.1 reduce-scatter.6
  517.9 301.0 all-reduce.5
where the time goes:
time: 862 us; the launch traced here: 855 us
  waiting for transfers between devices  424 us (49%)
  local copies, waits for them, and re-layouts  161 us (19%)
  matrix products  118 us (14%)
  other arithmetic  68.6 us (8%)
  blocking collectives  67.3 us (8%)
  between operations  15.2 us (2%)
    psum x1, waiting for transfers between devices, total_sum(): return lax.psum(values.astype(jnp.bfloat16), 'replica').astype(jnp.float32)  215 us
    all_gather x4, waiting for transfers between devices, gather(): return lax.all_gather(values, 'group', axis=0, tiled=True)  121 us
    unnamed x95, local copies, waits for them, and re-layouts  93.4 us
    reduce_scatter x4, waiting for transfers between devices, scatter(): lax.psum_scatter(values.astype(jnp.bfloat16), 'group', scatter_dimension=...  86.4 us
    psum x1, blocking collectives, local(): lax.psum(jnp.stack([gain_one_grad, gain_two_grad]), ('replica', 'group'))  39.4 us
    dot_general x7, matrix products, cols_dot(): lax.dot_general(left, right, (((1,), (1,)), ((), ())), preferred_element_...  31.9 us
    reshape x1, local copies, waits for them, and re-layouts, fold_offsets(): flattened.reshape(block_heads, row_count, row_count + col_count + 1)  31.4 us
    dot_general x7, matrix products, plain_dot(): return jnp.dot(left, right, preferred_element_type=jnp.float32)  31 us
  transfers between devices with their start and end apart: 9, of which 6 were waited for; matrix products, arithmetic and copies ran while one was open for 26% of the time, Pallas kernels for 0%

commit v1 on v0

--- a/solution.py
+++ b/solution.py
@@ -128,7 +128,9 @@
     up_grad = rows_dot(normed_two, grad_up)
 
     def total_sum(values):
-        return lax.psum(values.astype(jnp.bfloat16), "replica").astype(jnp.float32)
+        return jnp.sum(lax.all_gather(values.astype(jnp.bfloat16), "replica"), axis=0).astype(
+            jnp.float32
+        )
 
     ffn_out_grad, gate_grad, up_grad = (
         total_sum(ffn_out_grad),

time: 862 us -> 1530 us (1.77)
  waiting for transfers between devices: 424 us -> 976 us
  other arithmetic: 68.6 us -> 170 us
    all_gather x0 -> x7, waiting for transfers between devices: none -> 767 us  [total_sum(): lax.all_gather(values.astype(jnp.bfloat16), 'replica')]
    psum x1 -> x0, waiting for transfers between devices: 215 us -> none  [total_sum(): return lax.psum(values.astype(jnp.bfloat16), 'replica').astype(jnp.float32)]
    reduce_sum x0 -> x7, other arithmetic: none -> 99.3 us  [total_sum(): jnp.sum(lax.all_gather(values.astype(jnp.bfloat16), 'replica'), axis=0)]
    unnamed x95 -> x79, local copies, waits for them, and re-layouts: 93.4 us -> 95.3 us
  transfers between devices with their start and end apart: 9 -> 15, of which waited for: 6 -> 11; matrix products, arithmetic and copies ran while one was open for 26% -> 21% of each run, Pallas kernels for 0% -> 0%
where the time goes in v1:
time: 1530 us; the launch traced here: 1520 us
  waiting for transfers between devices  976 us (64%)
  other arithmetic  170 us (11%)
  local copies, waits for them, and re-layouts  163 us (11%)
  matrix products  125 us (8%)
  blocking collectives  68 us (4%)
  between operations  15.5 us (1%)
    all_gather x7, waiting for transfers between devices, total_sum(): lax.all_gather(values.astype(jnp.bfloat16), 'replica')  767 us
    all_gather x4, waiting for transfers between devices, gather(): return lax.all_gather(values, 'group', axis=0, tiled=True)  121 us
    reduce_sum x7, other arithmetic, total_sum(): jnp.sum(lax.all_gather(values.astype(jnp.bfloat16), 'replica'), axis=0)  99.3 us
    unnamed x79, local copies, waits for them, and re-layouts  95.3 us
    reduce_scatter x4, waiting for transfers between devices, scatter(): lax.psum_scatter(values.astype(jnp.bfloat16), 'group', scatter_dimension=...  86.4 us
    psum x1, blocking collectives, local(): lax.psum(jnp.stack([gain_one_grad, gain_two_grad]), ('replica', 'group'))  39.1 us
    dot_general x7, matrix products, rows_dot(): lax.dot_general(left, right, (((0,), (0,)), ((), ())), preferred_element_...  35.8 us
    dot_general x7, matrix products, cols_dot(): lax.dot_general(left, right, (((1,), (1,)), ((), ())), preferred_element_...  31.9 us
  transfers between devices with their start and end apart: 15, of which 11 were waited for; matrix products, arithmetic and copies ran while one was open for 21% of the time, Pallas kernels for 0%

profile of v1, /device:TPU:0, one launch (start us, length us, event | category | flops | bytes accessed | tf_op | source)
XLA Modules:
  0.0 1519.6 jit_solution(12938002518708547528)
XLA Ops:
  11.1 7.7 broadcast_in_dim.67
  18.8 25.5 %reshape.157 = f32[4198400]{0:T(1024)} reshape(f32[8,512,1025]{2,1,0:T(8,128)} %broadcast_in_dim.67) | data formatting | bytes 33587200
  44.3 16.5 %reshape.135 = f32[8,524800]{1,0:T(8,128)} reshape(f32[4198400]{0:T(1024)} %reshape.157) | data formatting | bytes 33587200 | tf_op jit(solution)/shard_map/reshape | solution.py:40
  60.8 5.8 slice-done
  66.6 16.0 %copy.45 = f32[1,8,512,1024]{3,2,1,0:T(8,128)S(1)} copy(f32[1,8,512,1024]{3,1,2,0:T(8,128)S(1)} %bitcast.133) | data formatting | bytes 33554432
  82.6 4.4 slice.30
  87.0 9.1 copy.40
  96.1 14.0 all_gather.58
  112.3 3.8 convolution_convert_fusion.13
  120.7 5.0 fusion.52
  129.0 8.0 fusion.15
  137.1 2.6 convolution_convert_fusion.8
  139.7 43.8 %reduce-scatter.5.cloned.1.call-done = bf16[128,2048]{1,0:T(8,128)(2,1)} async-done(((bf16[512,2048]{1,0:T(8,128)(2,1)}), bf16[128,2048]{1,0:T(8,128)(2,1)}) %reduce-scatter.5.cloned.1.call-update) | async-done | bytes 524304 | tf_op jit(solution)/shard_map/reduce_scatter | solution.py:87
  187.7 44.6 %all-gather.21.cloned.1.call-done = bf16[512,2048]{1,0:T(8,128)(2,1)} async-done(((bf16[128,2048]{1,0:T(8,128)(2,1)}), bf16[512,2048]{1,0:T(8,128)(2,1)}) %all-gather.21.cloned.1.call-update) | async-done | bytes 2097168 | tf_op jit(solution)/shard_map/all_gather | solution.py:84
  232.3 7.6 fusion.54
  239.9 7.1 fusion.53
  247.0 31.5 %all-gather.27.cloned.1.call-done = bf16[1,512,2048]{2,1,0:T(8,128)(2,1)} async-done(((bf16[1,128,2048]{2,1,0:T(8,128)(2,1)}), bf16[1,512,2048]{2,1,0:T(8,128)(2,1)}) %all-gather.27.cloned.1.call-update) | async-done | bytes 2097168 | tf_op jit(solution)/shard_map/all_gather | solution.py:84
  278.5 10.3 multiply_convert_fusion.1
  288.8 5.8 fusion.55
  294.7 6.7 add_convert_fusion.1
  301.5 42.6 %reduce-scatter.9.cloned.1.call-done = bf16[128,2048]{1,0:T(8,128)(2,1)} async-done(((bf16[512,2048]{1,0:T(8,128)(2,1)}), bf16[128,2048]{1,0:T(8,128)(2,1)}) %reduce-scatter.9.cloned.1.call-update) | async-done | bytes 524304 | tf_op jit(solution)/shard_map/reduce_scatter | solution.py:87
  348.5 45.2 %all-gather.23.cloned.1.call-done = bf16[512,2048]{1,0:T(8,128)(2,1)} async-done(((bf16[128,2048]{1,0:T(8,128)(2,1)}), bf16[512,2048]{1,0:T(8,128)(2,1)}) %all-gather.23.cloned.1.call-update) | async-done | bytes 2097168 | tf_op jit(solution)/shard_map/all_gather | solution.py:84
  393.6 3.7 convolution_convert_fusion.11
  397.3 8.2 fusion.18
  405.5 4.8 multiply_reduce_fusion
  420.3 2.7 add_convert_fusion
  423.5 7.1 convolution_convert_fusion.7
  430.8 4.2 convolution_convert_fusion.3
  435.0 4.4 convolution_convert_fusion.4
  439.5 4.5 convolution_convert_fusion.5
  444.0 4.6 convolution_convert_fusion.6
  448.6 6.3 convolution_convert_fusion
  456.6 6.0 convolution_convert_fusion.1
  462.8 6.0 convolution_convert_fusion.2
  468.8 6.5 copy.41
  475.3 6.7 pad_bitcast_fusion
  482.0 11.5 copy.43
  493.6 9.9 pad_convert_fusion
  503.5 12.8 reshape.159
  516.3 30.8 %reshape.144 = f32[8,512,1025]{2,1,0:T(8,128)} reshape(f32[4198400]{0:T(1024)} %reshape.159) | data formatting | bytes 33587200 | tf_op jit(solution)/shard_map/reshape | solution.py:52
  547.1 7.4 reduce_sum.207
  554.9 14.8 psum.15
  571.3 39.1 %psum.14 = f32[2,2048]{1,0:T(2,128)S(1)} all-reduce(f32[2,2048]{1,0:T(2,128)S(1)} %pad_maximum_fusion), channel_id=1, replica_groups=mesh['replica'=8,'group'=4] {'replica','group'}, use_global_device_ids=true, to_apply=%region_14.15 | all-reduce | flops 4096 | bytes 32768 | tf_op jit(solution)/shard_map/psum | solution.py:187
  611.2 3.2 fusion.34
  614.4 10.0 reduce_sum.206
  624.4 2.5 convert_element_type.224
  626.9 68.8 %all-gather.33.cloned.1.call-done = bf16[16384,512]{1,0:T(8,128)(2,1)} async-done(((bf16[2048,512]{1,0:T(8,128)(2,1)}), bf16[16384,512]{1,0:T(8,128)(2,1)}) %all-gather.33.cloned.1.call-update) | async-done | bytes 16777232 | tf_op jit(solution)/shard_map/all_gather | solution.py:131
  695.7 9.3 reduce_sum.205
  705.0 2.6 convert_element_type.222
  707.6 79.8 %all-gather.31.cloned.1.call-done = bf16[16384,512]{1,0:T(8,128)(2,1)} async-done(((bf16[2048,512]{1,0:T(8,128)(2,1)}), bf16[16384,512]{1,0:T(8,128)(2,1)}) %all-gather.31.cloned.1.call-update) | async-done | bytes 16777232 | tf_op jit(solution)/shard_map/all_gather | solution.py:131
  787.5 9.4 reduce_sum.204
  796.9 82.2 %all-gather.29.cloned.1.call-done = bf16[16384,512]{1,0:T(8,128)(2,1)} async-done(((bf16[2048,512]{1,0:T(8,128)(2,1)}), bf16[16384,512]{1,0:T(8,128)(2,1)}) %all-gather.29.cloned.1.call-update) | async-done | bytes 16777232 | tf_op jit(solution)/shard_map/all_gather | solution.py:131
  879.1 10.9 reduce_sum.203
  890.0 4.8 convert_element_type.218
  894.7 3.4 convert_element_type.220
  898.1 180.1 %all-gather.41.cloned.1.call-done = bf16[10240,2048]{1,0:T(8,128)(2,1)} async-done(((bf16[1280,2048]{1,0:T(8,128)(2,1)}), bf16[10240,2048]{1,0:T(8,128)(2,1)}) %all-gather.41.cloned.1.call-update) | async-done | bytes 41943056 | tf_op jit(solution)/shard_map/all_gather | solution.py:131
  1078.2 21.0 %reduce_sum.210 = bf16[1280,2048]{1,0:T(8,128)(2,1)} reduce(bf16[8,1280,2048]{2,1,0:T(8,128)(2,1)} %bitcast.134, bf16[]{:T(256)} %constant.48.clone.1), dimensions={0}, to_apply=%region_23.24 | reduce | flops 18350080 | bytes 47185920 | tf_op jit(solution)/shard_map/reduce_sum | solution.py:131
  1099.1 178.0 %all-gather.39.cloned.1.call-done = bf16[16384,1280]{1,0:T(8,128)(2,1)} async-done(((bf16[2048,1280]{1,0:T(8,128)(2,1)}), bf16[16384,1280]{1,0:T(8,128)(2,1)}) %all-gather.39.cloned.1.call-update) | async-done | bytes 41943056 | tf_op jit(solution)/shard_map/all_gather | solution.py:131
  1277.1 21.0 %reduce_sum.209 = bf16[2048,1280]{1,0:T(8,128)(2,1)} reduce(bf16[8,2048,1280]{2,1,0:T(8,128)(2,1)} %bitcast.135, bf16[]{:T(256)} %constant.48.clone.1), dimensions={0}, to_apply=%region_22.23 | reduce | flops 18350080 | bytes 47185920 | tf_op jit(solution)/shard_map/reduce_sum | solution.py:131
  1298.1 178.5 %all-gather.37.cloned.1.call-done = bf16[16384,1280]{1,0:T(8,128)(2,1)} async-done(((bf16[2048,1280]{1,0:T(8,128)(2,1)}), bf16[16384,1280]{1,0:T(8,128)(2,1)}) %all-gather.37.cloned.1.call-update) | async-done | bytes 41943056 | tf_op jit(solution)/shard_map/all_gather | solution.py:131
  1476.6 17.7 %reduce_sum.208 = bf16[2048,1280]{1,0:T(8,128)(2,1)} reduce(bf16[8,2048,1280]{2,1,0:T(8,128)(2,1)} %bitcast.136, bf16[]{:T(256)} %constant.48.clone.1), dimensions={0}, to_apply=%region_21.22 | reduce | flops 18350080 | bytes 47185920 | tf_op jit(solution)/shard_map/reduce_sum | solution.py:131
  1494.3 7.9 convert_element_type.226
  1502.2 4.9 convert_element_type.228
  1507.1 5.5 convert_element_type.230
  (140 shorter events, 37.0 us)
Async XLA Ops:
  7.2 129.9 %copy-start = (bf16[512,2048]{1,0:T(8,128)(2,1)S(1)}, bf16[512,2048]{1,0:T(8,128)(2,1)}, u32[]{:S(2)}) copy-start(bf16[512,2048]{1,0:T(8,128)(2,1)} %param.21) | copy-start | bytes 6291460
  7.2 103.0 %all-gather.25.cloned.1.call-start = ((), (), s32[]{:S(2)}) async-start(), calls=%async_computation.10 | async-start | bytes 2621440 | tf_op jit(solution)/shard_map/all_gather | solution.py:84
  7.9 175.6 %reduce-scatter.5.cloned.1.call-start = ((), (), s32[]{:S(2)}) async-start(), calls=%async_computation.4 | async-start | bytes 2621440 | tf_op jit(solution)/shard_map/reduce_scatter | solution.py:87
  60.8 5.8 slice-start
  112.3 3.8 copy-start.15
  112.3 3.8 copy-start.16
  112.3 6.1 slice-start.3
  116.1 1.5 copy-start.13
  116.1 2.6 slice-start.4
  117.6 0.8 copy-start.11
  120.7 6.1 copy-start.3
  120.7 6.1 copy-start.9
  128.2 0.8 copy-start.24
  137.0 47.8 %copy-start.22 = (bf16[8,64,512]{2,1,0:T(8,128)(2,1)}, bf16[8,64,512]{2,1,0:T(8,128)(2,1)S(1)}, u32[]{:S(2)}) copy-start(bf16[8,64,512]{2,1,0:T(8,128)(2,1)S(1)} %fusion.15) | copy-start | bytes 1572868
  137.0 46.5 %copy-start.4 = (bf16[1,128,2048]{2,1,0:T(8,128)(2,1)S(1)}, bf16[1,128,2048]{2,1,0:T(8,128)(2,1)}, u32[]{:S(2)}) copy-start(bf16[1,128,2048]{2,1,0:T(8,128)(2,1)} %param.14) | copy-start | bytes 1572868
  139.7 92.6 %all-gather.21.cloned.1.call-start = ((), (), s32[]{:S(2)}) async-start(), calls=%async_computation.5 | async-start | bytes 2621440 | tf_op jit(solution)/shard_map/all_gather | solution.py:84
  186.9 91.6 %all-gather.27.cloned.1.call-start = ((), (), s32[]{:S(2)}) async-start(), calls=%async_computation.11 | async-start | bytes 2621440 | tf_op jit(solution)/shard_map/all_gather | solution.py:84
  187.5 156.6 %reduce-scatter.9.cloned.1.call-start = ((), (), s32[]{:S(2)}) async-start(), calls=%async_computation.7 | async-start | bytes 2621440 | tf_op jit(solution)/shard_map/reduce_scatter | solution.py:87
  232.3 7.6 copy-start.19
  288.8 5.8 copy-start.28
  288.8 5.8 copy-start.27
  294.7 49.4 %copy-start.6 = (bf16[128,2048]{1,0:T(8,128)(2,1)S(1)}, bf16[128,2048]{1,0:T(8,128)(2,1)}, u32[]{:S(2)}) copy-start(bf16[128,2048]{1,0:T(8,128)(2,1)} %reduce-scatter.5.cloned.1.call-done) | copy-start | bytes 1572868
  301.4 92.2 %all-gather.23.cloned.1.call-start = ((), (), s32[]{:S(2)}) async-start(), calls=%async_computation.8 | async-start | bytes 2621440 | tf_op jit(solution)/shard_map/all_gather | solution.py:84
  348.2 221.5 %reduce-scatter.11.cloned.1.call-start = ((), (), s32[]{:S(2)}) async-start(), calls=%async_computation.9 | async-start | bytes 2621440 | tf_op jit(solution)/shard_map/reduce_scatter | solution.py:87
  397.3 8.2 copy-start.25
  397.3 8.2 copy-start.26
  405.5 4.9 slice-start.1
  405.5 5.8 slice-start.2
  411.4 2.5 copy-start.14
  413.9 2.2 copy-start.2
  413.9 1.4 copy-start.12
  413.9 3.3 copy-start.17
  417.2 1.6 copy-start.18
  418.7 1.6 copy-start.10
  423.1 188.1 %reduce-scatter.7.cloned.1.call-start = ((), (), s32[]{:S(2)}) async-start(), calls=%async_computation.6 | async-start | bytes 2621440 | tf_op jit(solution)/shard_map/reduce_scatter | solution.py:87
  423.5 7.2 copy-start.23
  430.7 183.7 %all-gather.35.cloned.1.call-start = ((), (), s32[]{:S(2)}) async-start(), calls=%async_computation.15 | async-start | bytes 18874368 | tf_op jit(solution)/shard_map/all_gather | solution.py:131
  435.0 260.7 %all-gather.33.cloned.1.call-start = ((), (), s32[]{:S(2)}) async-start(), calls=%async_computation.14 | async-start | bytes 18874368 | tf_op jit(solution)/shard_map/all_gather | solution.py:131
  439.4 348.1 %all-gather.31.cloned.1.call-start = ((), (), s32[]{:S(2)}) async-start(), calls=%async_computation.13 | async-start | bytes 18874368 | tf_op jit(solution)/shard_map/all_gather | solution.py:131
  443.9 4.7 copy-start.29
  444.0 435.2 %all-gather.29.cloned.1.call-start = ((), (), s32[]{:S(2)}) async-start(), calls=%async_computation.12 | async-start | bytes 18874368 | tf_op jit(solution)/shard_map/all_gather | solution.py:131
  448.6 629.6 %all-gather.41.cloned.1.call-start = ((), (), s32[]{:S(2)}) async-start(), calls=%async_computation.18 | async-start | bytes 47185920 | tf_op jit(solution)/shard_map/all_gather | solution.py:131
  455.0 1.6 copy-start.20
  455.0 822.1 %all-gather.39.cloned.1.call-start = ((), (), s32[]{:S(2)}) async-start(), calls=%async_computation.17 | async-start | bytes 47185920 | tf_op jit(solution)/shard_map/all_gather | solution.py:131
  462.6 1014.0 %all-gather.37.cloned.1.call-start = ((), (), s32[]{:S(2)}) async-start(), calls=%async_computation.16 | async-start | bytes 47185920 | tf_op jit(solution)/shard_map/all_gather | solution.py:131
  547.1 7.4 copy-start.21
  547.1 64.1 %copy-start.7 = (bf16[128,2048]{1,0:T(8,128)(2,1)S(1)}, bf16[128,2048]{1,0:T(8,128)(2,1)}, u32[]{:S(2)}) copy-start(bf16[128,2048]{1,0:T(8,128)(2,1)} %reduce-scatter.9.cloned.1.call-done) | copy-start | bytes 1572868
  547.1 64.1 %copy-start.8 = (bf16[1,128,2048]{2,1,0:T(8,128)(2,1)S(1)}, bf16[1,128,2048]{2,1,0:T(8,128)(2,1)}, u32[]{:S(2)}) copy-start(bf16[1,128,2048]{2,1,0:T(8,128)(2,1)} %param.27) | copy-start | bytes 1572868
  1494.3 7.9 copy-start.5
  1494.3 12.8 slice-start.5
  1502.2 4.9 slice-start.6
  1502.2 10.4 copy-start.1
Sparse Core Ops, SparseCore 0:
  9.6 48.6 all-gather.24
  139.8 43.6 reduce-scatter.4
  187.0 45.2 all-gather.20
  233.8 44.6 all-gather.26
  301.5 42.4 reduce-scatter.8
  348.3 45.2 all-gather.22
  423.2 42.5 reduce-scatter.10
  468.8 43.1 reduce-scatter.6
  513.9 90.1 all-gather.34
  605.8 89.8 all-gather.32
  697.6 89.8 all-gather.30
  789.2 89.8 all-gather.28
  881.0 197.1 all-gather.40
  1079.9 197.1 all-gather.38
  1279.4 197.1 all-gather.36
